TPU v7x, 512 devices: a whole 4x8x8 slice. The times are simulated.
512 devices in a mesh: gx: 64 (over x, z_lo, y), gy: 8 (over z_hi, core).
Axes of the slice: x: 4, y: 8, z: 8 (z_hi: 4, z_lo: 2; z = z_hi * 2 + z_lo), core: 2. Of those that a mesh axis runs over, the one named last changes fastest.
Arguments:
- flow_field: bfloat16 [256, 128, 64, 128], P('gx', 'gy'), may hold values from -6 to 6
- spectral_weight: bfloat16 [512, 64, 2, 64, 128], P(('gy', 'gx')), may hold values from -1 to 1
- conv_weight: bfloat16 [3, 3, 3, 128, 128], replicated, may hold values from -0.109375 to 0.109375
- channel_bias: float32 [128], replicated, may hold values from -3 to 3
Outputs:
- activated: bfloat16 [256, 128, 64, 128], P('gx', 'gy')
All inputs are finite; a program needn't handle non-finite values.
Results may differ from a plain program's by a relative error of at most 0.018.
Values may be sent and summed in bfloat16 or wider, within the bound.
A program may use at most 128 MiB of HBM per device.

v0:
```python
import math
import jax
import jax.numpy as jnp
from jax import lax
from jax.sharding import PartitionSpec as P

MX = 64
MY = 16
MZ = 16


def with_halo(array, sides, width):
    for axis, dim in sides:
        size, length = (lax.axis_size(axis), array.shape[dim])
        up = [(i, (i + 1) % size) for i in range(size - 1)]
        down = [(j, i) for i, j in up]
        last = lax.slice_in_dim(array, length - width, length, axis=dim)
        initial = lax.slice_in_dim(array, 0, width, axis=dim)
        before = lax.ppermute(last, axis, up)
        after = lax.ppermute(initial, axis, down)
        array = jnp.concatenate([before, array, after], axis=dim)
    return array


def signed_modes(mode_count):
    position = jnp.arange(mode_count, dtype=jnp.int32)
    return jnp.where(position < mode_count // 2, position, position - mode_count)


def angle_grid(first, second, length):
    phase_turns = first[:, None] * second[None, :] % length
    return phase_turns.astype(jnp.float32) * (2.0 * math.pi / length)


def real_table(first, second, length, factor):
    angles = angle_grid(first, second, length)
    return jnp.stack([jnp.cos(angles) * factor, -jnp.sin(angles) * factor])


def complex_table(first, second, length, factor, direction):
    angles = angle_grid(first, second, length)
    cosine = jnp.cos(angles) * factor
    sine_part = jnp.sin(angles) * factor
    return jnp.stack(
        [jnp.stack([cosine, direction * sine_part]), jnp.stack([-direction * sine_part, cosine])]
    )


def spectral_part(flow_field, spectral_weight):
    highest = lax.Precision.HIGHEST
    cells_x, cells_y, cells_z, channels = flow_field.shape
    count_x = lax.axis_size("gx")
    count_y = lax.axis_size("gy")
    full_x = cells_x * count_x
    full_y = cells_y * count_y
    item_count = spectral_weight.shape[0]
    local_y = lax.axis_index("gy") * cells_y + jnp.arange(cells_y, dtype=jnp.int32)
    grid_x = jnp.arange(full_x, dtype=jnp.int32)
    grid_z = jnp.arange(cells_z, dtype=jnp.int32)
    modes_z = jnp.arange(MZ, dtype=jnp.int32)
    forward_z = real_table(grid_z, modes_z, cells_z, cells_z ** (-0.5)).astype(jnp.bfloat16)
    z_spectrum = jnp.einsum(
        "xyzc,pzk->pxykc", flow_field, forward_z, preferred_element_type=jnp.float32
    )
    forward_y = complex_table(local_y, signed_modes(MY), full_y, full_y ** (-0.5), -1.0)
    y_partial = jnp.einsum("pxykc,pqyj->qxjkc", z_spectrum, forward_y, precision=highest)
    y_partial = y_partial.reshape(2, cells_x, count_y, count_x, item_count, channels // 2)
    owned = lax.psum_scatter(
        y_partial.astype(jnp.bfloat16), "gy", scatter_dimension=2, tiled=True
    ).astype(jnp.float32)
    owned_modes = owned.reshape(2, cells_x, count_x, item_count, channels // 2)
    gathered_rows = lax.all_to_all(
        owned_modes.astype(jnp.bfloat16), "gx", split_axis=2, concat_axis=1, tiled=True
    ).astype(owned_modes.dtype)
    gathered_rows = gathered_rows.reshape(2, full_x, item_count, channels // 2)
    forward_x = complex_table(grid_x, signed_modes(MX), full_x, full_x ** (-0.5), -1.0)
    x_spectrum = jnp.einsum("pxjc,pqxm->qmjc", gathered_rows, forward_x, precision=highest).astype(
        jnp.bfloat16
    )
    products = jnp.einsum(
        "pmjc,jmqco->pqmjo", x_spectrum, spectral_weight, preferred_element_type=jnp.float32
    )
    mixed_modes = jnp.stack([products[0, 0] - products[1, 1], products[0, 1] + products[1, 0]])
    backward_x = complex_table(signed_modes(MX), grid_x, full_x, MX ** (-0.5), 1.0)
    inverse_x = jnp.einsum("pmjc,pqmx->qxjc", mixed_modes, backward_x, precision=highest)
    inverse_x = inverse_x.reshape(2, full_x, 1, item_count, channels)
    returned = lax.all_to_all(
        inverse_x.astype(jnp.bfloat16), "gx", split_axis=1, concat_axis=2, tiled=True
    ).astype(inverse_x.dtype)
    band_rows = MY // count_y
    summed = returned.reshape(2, cells_x, band_rows * MZ, 2, channels).sum(axis=3)
    summed = summed.reshape(2, cells_x, band_rows, MZ, channels)
    coefficients = lax.all_gather(summed.astype(jnp.bfloat16), "gy", axis=2, tiled=True).astype(
        summed.dtype
    )
    backward_y = complex_table(signed_modes(MY), local_y, full_y, MY ** (-0.5), 1.0)
    y_inverse = jnp.einsum("pxjkc,pqjy->qxykc", coefficients, backward_y, precision=highest).astype(
        jnp.bfloat16
    )
    backward_z = real_table(modes_z, grid_z, cells_z, MZ ** (-0.5)).astype(jnp.bfloat16)
    return jnp.einsum("pxykc,pkz->xyzc", y_inverse, backward_z, preferred_element_type=jnp.float32)


def convolve(flow_field, conv_weight):
    cells_x, cells_y, cells_z, channels = flow_field.shape
    padded = with_halo(flow_field, (("gx", 0), ("gy", 1)), 1)
    padded = jnp.pad(padded, ((0, 0), (0, 0), (1, 1), (0, 0)))
    stacked = jnp.concatenate(
        [padded[:, :, 0:cells_z], padded[:, :, 1 : cells_z + 1], padded[:, :, 2 : cells_z + 2]],
        axis=3,
    )
    kernel = conv_weight.reshape(3, 3, 3 * channels, channels)
    accumulated = jnp.zeros((cells_x, cells_y, cells_z, channels), jnp.float32)
    for shift_x in range(3):
        for shift_y in range(3):
            accumulated = accumulated + jnp.dot(
                stacked[shift_x : shift_x + cells_x, shift_y : shift_y + cells_y],
                kernel[shift_x, shift_y],
                preferred_element_type=jnp.float32,
            )
    return accumulated


def body(flow_field, spectral_weight, conv_weight, channel_bias):
    convolved = convolve(flow_field, conv_weight)
    spectral = spectral_part(flow_field, spectral_weight)
    return jax.nn.gelu(spectral + convolved + channel_bias, approximate=True).astype(jnp.bfloat16)


def solution(mesh):
    placed = (P("gx", "gy", None, None), P(("gy", "gx"), None, None, None, None), P(), P())
    return jax.shard_map(
        body, mesh=mesh, in_specs=placed, out_specs=P("gx", "gy", None, None), check_vma=False
    )
```

profile of v0, /device:TPU:1, one launch (start us, length us, event | category | flops | bytes accessed | tf_op | source)
XLA Modules:
  0.0 191.2 jit_solution(16741173766615642969)
XLA Ops:
  6.5 2.0 %fusion.100 = (bf16[1,16,64,128]{3,2,1,0:T(8,128)(2,1)}, bf16[1,16,64,128]{3,2,1,0:T(8,128)(2,1)}) fusion(bf16[4,16,64,128]{3,2,1,0:T(8,128)(2,1)} %param.4), kind=kLoop, calls=%fused_computation.177 | loop fusion | bytes 1048576 | tf_op jit(solution)/shard_map/slice | solution.py:18
  9.9 5.4 %collective-permute-start = (bf16[1,16,64,128]{3,2,1,0:T(8,128)(2,1)}, bf16[1,16,64,128]{3,2,1,0:T(8,128)(2,1)}, u32[]{:S(2)}, u32[]{:S(2)}) collective-permute-start(bf16[1,16,64,128]{3,2,1,0:T(8,128)(2,1)} %get-tuple-element.10), channel_id=1, source_target_pairs={{0,8},{8,16},{16,24},{24,32},{32,40},{40,48},{48,56},{56,64},{64,7... | collective-permute-start | bytes 786440 | tf_op jit(solution)/shard_map/ppermute | solution.py:19
  16.1 1.5 convolution_bitcast_fusion.2
  19.8 2.5 %convert_element_type.204 = bf16[2,4,8,64,1,64]{5,3,2,1,0,4:T(8,128)(2,1)} reshape(bf16[2,4,16,16,128]{4,3,2,1,0:T(8,128)(2,1)} %copy.48) | data formatting | bytes 1048576 | tf_op jit(solution)/shard_map/convert_element_type | solution.py:69
  28.5 7.1 %collective-permute-start.2 = (bf16[6,1,64,128]{3,2,1,0:T(8,128)(2,1)S(1)}, bf16[6,1,64,128]{3,2,1,0:T(8,128)(2,1)S(1)}, u32[]{:S(2)}, u32[]{:S(2)}) collective-permute-start(bf16[6,1,64,128]{3,2,1,0:T(8,128)(2,1)S(1)} %get-tuple-element.7), channel_id=1, source_target_pairs={{0,1},{1,2},{2,3},{3,4},{4,5},{5,6},{6,7},{8,9},{9,10},{10,11},{11... | collective-permute-start | bytes 294920 | tf_op jit(solution)/shard_map/ppermute | solution.py:19
  35.6 2.9 %collective-permute-start.3 = (bf16[6,1,64,128]{3,2,1,0:T(8,128)(2,1)S(1)}, bf16[6,1,64,128]{3,2,1,0:T(8,128)(2,1)S(1)}, u32[]{:S(2)}, u32[]{:S(2)}) collective-permute-start(bf16[6,1,64,128]{3,2,1,0:T(8,128)(2,1)S(1)} %get-tuple-element.8), channel_id=1, source_target_pairs={{1,0},{2,1},{3,2},{4,3},{5,4},{6,5},{7,6},{9,8},{10,9},{11,10},{12... | collective-permute-start | bytes 294920 | tf_op jit(solution)/shard_map/ppermute | solution.py:20
  39.1 3.3 %collective-permute-done.3 = bf16[6,1,64,128]{3,2,1,0:T(8,128)(2,1)S(1)} collective-permute-done((bf16[6,1,64,128]{3,2,1,0:T(8,128)(2,1)S(1)}, bf16[6,1,64,128]{3,2,1,0:T(8,128)(2,1)S(1)}, u32[]{:S(2)}, u32[]{:S(2)}) %collective-permute-start.3) | collective-permute-done | bytes 98336 | tf_op jit(solution)/shard_map/ppermute | solution.py:20
  45.8 2.7 %fusion.41 = f32[4,16,64,128]{3,2,1,0:T(8,128)} fusion(bf16[6,18,64,384]{3,2,1,0:T(8,128)(2,1)S(1)} %pad_maximum_fusion, bf16[3,3,384,128]{3,2,1,0:T(8,128)(2,1)S(1)} %bitcast.222), kind=kOutput, calls=%fused_computation.56 | convolution fusion | flops 402653184 | bytes 7503872 | tf_op jit(solution)/shard_map/dot_general | solution.py:116
  48.5 2.3 %fusion.42 = f32[4,16,64,128]{3,2,1,0:T(8,128)} fusion(bf16[6,18,64,384]{3,2,1,0:T(8,128)(2,1)S(1)} %pad_maximum_fusion, bf16[3,3,384,128]{3,2,1,0:T(8,128)(2,1)S(1)} %bitcast.223), kind=kOutput, calls=%fused_computation.58 | convolution fusion | flops 402653184 | bytes 7503872 | tf_op jit(solution)/shard_map/dot_general | solution.py:116
  50.8 2.3 %fusion.43 = f32[4,16,64,128]{3,2,1,0:T(8,128)} fusion(bf16[6,18,64,384]{3,2,1,0:T(8,128)(2,1)S(1)} %pad_maximum_fusion, bf16[3,3,384,128]{3,2,1,0:T(8,128)(2,1)S(1)} %bitcast.224), kind=kOutput, calls=%fused_computation.60 | convolution fusion | flops 402653184 | bytes 7503872 | tf_op jit(solution)/shard_map/dot_general | solution.py:116
  53.1 2.4 %fusion.44 = f32[4,16,64,128]{3,2,1,0:T(8,128)} fusion(bf16[6,18,64,384]{3,2,1,0:T(8,128)(2,1)S(1)} %pad_maximum_fusion, bf16[3,3,384,128]{3,2,1,0:T(8,128)(2,1)S(1)} %bitcast.225), kind=kOutput, calls=%fused_computation.62 | convolution fusion | flops 402653184 | bytes 7503872 | tf_op jit(solution)/shard_map/dot_general | solution.py:116
  55.5 2.3 %fusion.45 = f32[4,16,64,128]{3,2,1,0:T(8,128)} fusion(bf16[6,18,64,384]{3,2,1,0:T(8,128)(2,1)S(1)} %pad_maximum_fusion, bf16[3,3,384,128]{3,2,1,0:T(8,128)(2,1)S(1)} %bitcast.226), kind=kOutput, calls=%fused_computation.64 | convolution fusion | flops 402653184 | bytes 7503872 | tf_op jit(solution)/shard_map/dot_general | solution.py:116
  57.8 2.4 %fusion.46 = f32[4,16,64,128]{3,2,1,0:T(8,128)} fusion(bf16[6,18,64,384]{3,2,1,0:T(8,128)(2,1)S(1)} %pad_maximum_fusion, bf16[3,3,384,128]{3,2,1,0:T(8,128)(2,1)S(1)} %bitcast.227), kind=kOutput, calls=%fused_computation.66 | convolution fusion | flops 402653184 | bytes 7503872 | tf_op jit(solution)/shard_map/dot_general | solution.py:116
  60.2 49.9 %all-reduce.4.cloned.1.call-done = bf16[2,4,8,64,1,64]{5,3,2,1,0,4:T(8,128)(2,1)} async-done(((bf16[2,4,8,64,1,64]{5,3,2,1,0,4:T(8,128)(2,1)}), bf16[2,4,8,64,1,64]{5,3,2,1,0,4:T(8,128)(2,1)}) %all-reduce.4.cloned.1.call-update) | async-done | bytes 524304
  112.4 1.7 reshape.950
  114.1 10.7 %all-to-all-start = ((bf16[64,2,256]{2,1,0:T(2,128)(2,1)}), bf16[64,2,256]{2,1,0:T(2,128)(2,1)}, u32[]{:S(2)}, u32[]{:S(2)}) async-start(bf16[64,2,256]{2,1,0:T(2,128)(2,1)} %reshape.950), calls=%async_computation | async-start | bytes 131072 | tf_op jit(solution)/shard_map/all_to_all | solution.py:72
  124.8 4.2 %fusion.47 = f32[4,16,64,128]{3,2,1,0:T(8,128)} fusion(bf16[6,18,64,384]{3,2,1,0:T(8,128)(2,1)} %copy-done.1, bf16[3,3,384,128]{3,2,1,0:T(8,128)(2,1)S(1)} %bitcast.228), kind=kOutput, calls=%fused_computation.68 | convolution fusion | flops 402653184 | bytes 7503872 | tf_op jit(solution)/shard_map/dot_general | solution.py:116
  129.0 4.9 %all-to-all-done = bf16[64,2,256]{2,1,0:T(2,128)(2,1)} async-done(((bf16[64,2,256]{2,1,0:T(2,128)(2,1)}), bf16[64,2,256]{2,1,0:T(2,128)(2,1)}, u32[]{:S(2)}, u32[]{:S(2)}) %all-to-all-start) | async-done | bytes 65568 | tf_op jit(solution)/shard_map/all_to_all | solution.py:72
  134.0 1.7 reshape.951
  138.8 5.7 %all-to-all-start.1 = ((bf16[2,256,1,1,128]{4,0,3,2,1:T(2,128)(2,1)}), bf16[2,256,1,1,128]{4,0,3,2,1:T(2,128)(2,1)S(1)}, u32[]{:S(2)}, u32[]{:S(2)}) async-start(bf16[2,256,1,1,128]{4,0,3,2,1:T(2,128)(2,1)} %copy.55), calls=%async_computation.1 | async-start | bytes 262144 | tf_op jit(solution)/shard_map/all_to_all | solution.py:87
  144.5 4.2 %fusion.48 = f32[4,16,64,128]{3,2,1,0:T(8,128)} fusion(bf16[6,18,64,384]{3,2,1,0:T(8,128)(2,1)} %copy-done.1, bf16[3,3,384,128]{3,2,1,0:T(8,128)(2,1)S(1)} %bitcast.229), kind=kOutput, calls=%fused_computation.70 | convolution fusion | flops 402653184 | bytes 7503872 | tf_op jit(solution)/shard_map/dot_general | solution.py:116
  148.7 5.8 %all-to-all-done.1 = bf16[2,256,1,1,128]{4,0,3,2,1:T(2,128)(2,1)S(1)} async-done(((bf16[2,256,1,1,128]{4,0,3,2,1:T(2,128)(2,1)}), bf16[2,256,1,1,128]{4,0,3,2,1:T(2,128)(2,1)S(1)}, u32[]{:S(2)}, u32[]{:S(2)}) %all-to-all-start.1) | async-done | bytes 131104 | tf_op jit(solution)/shard_map/all_to_all | solution.py:87
  154.7 19.6 %all_gather.3 = bf16[2,4,16,16,128]{4,3,1,0,2:T(8,128)(2,1)S(1)} all-gather(bf16[2,4,2,16,128]{4,3,1,0,2:T(8,128)(2,1)S(1)} %copy.58), channel_id=1, replica_groups=mesh['gx'=64,'gy'=8] {'gy'}, dimensions={2}, use_global_device_ids=true | all-gather | bytes 589824 | tf_op jit(solution)/shard_map/all_gather | solution.py:93
  175.6 8.8 %fusion.11 = bf16[4,16,64,128]{3,2,1,0:T(8,128)(2,1)} fusion(f32[64,4,16,128,1]{3,0,4,2,1:T(8,128)S(1)} %fusion.32, f32[4,16,64,128]{3,2,1,0:T(8,128)S(1)} %copy-done.2, f32[4,16,64,128]{3,2,1,0:T(8,128)S(1)} %copy-done.3, f32[4,16,64,128]{3,2,1,0:T(8,128)} %fusion.43, f32[4,16,64,128]{3,2,1,0:T(8,128)} %fusion.44, f32[4,16,64,128]{3,2,1,0:T(8,128)} %fusion.45, ...), kind=kOutput, calls=%fused_computation.15 | convolution fusion | flops 412614656 | bytes 25330176 | tf_op jit(solution)/shard_map/dot_general | solution.py:116
  (64 shorter events, 21.2 us)
Async XLA Ops:
  6.5 130.4 %copy-start = (bf16[1,64,2,64,128]{4,3,2,1,0:T(8,128)(2,1)S(1)}, bf16[1,64,2,64,128]{4,3,2,1,0:T(8,128)(2,1)}, u32[]{:S(2)}) copy-start(bf16[1,64,2,64,128]{4,3,2,1,0:T(8,128)(2,1)} %param.5) | copy-start | bytes 6291460
  6.5 103.6 %all-reduce.4.cloned.1.call-start = ((), (), s32[]{:S(2)}) async-start(), calls=%async_computation.2 | async-start | bytes 2097152
  8.6 18.9 %collective-permute-start.1 = (bf16[1,16,64,128]{3,2,1,0:T(8,128)(2,1)}, bf16[1,16,64,128]{3,2,1,0:T(8,128)(2,1)}, u32[]{:S(2)}, u32[]{:S(2)}) collective-permute-start(bf16[1,16,64,128]{3,2,1,0:T(8,128)(2,1)} %get-tuple-element.9), channel_id=1, source_target_pairs={{8,0},{16,8},{24,16},{32,24},{40,32},{48,40},{56,48},{64,56},{72,6... | collective-permute-start | bytes 786440 | tf_op jit(solution)/shard_map/ppermute | solution.py:20
  9.9 16.5 %collective-permute-start = (bf16[1,16,64,128]{3,2,1,0:T(8,128)(2,1)}, bf16[1,16,64,128]{3,2,1,0:T(8,128)(2,1)}, u32[]{:S(2)}, u32[]{:S(2)}) collective-permute-start(bf16[1,16,64,128]{3,2,1,0:T(8,128)(2,1)} %get-tuple-element.10), channel_id=1, source_target_pairs={{0,8},{8,16},{16,24},{24,32},{32,40},{40,48},{48,56},{56,64},{64,7... | collective-permute-start | bytes 786440 | tf_op jit(solution)/shard_map/ppermute | solution.py:19
  19.8 7.5 %copy-start.4 = (bf16[4,16,64,128]{3,2,1,0:T(8,128)(2,1)S(1)}, bf16[4,16,64,128]{3,2,1,0:T(8,128)(2,1)}, u32[]{:S(2)}) copy-start(bf16[4,16,64,128]{3,2,1,0:T(8,128)(2,1)} %param.4) | copy-start | bytes 3145732
  28.5 10.6 %collective-permute-start.2 = (bf16[6,1,64,128]{3,2,1,0:T(8,128)(2,1)S(1)}, bf16[6,1,64,128]{3,2,1,0:T(8,128)(2,1)S(1)}, u32[]{:S(2)}, u32[]{:S(2)}) collective-permute-start(bf16[6,1,64,128]{3,2,1,0:T(8,128)(2,1)S(1)} %get-tuple-element.7), channel_id=1, source_target_pairs={{0,1},{1,2},{2,3},{3,4},{4,5},{5,6},{6,7},{8,9},{9,10},{10,11},{11... | collective-permute-start | bytes 294920 | tf_op jit(solution)/shard_map/ppermute | solution.py:19
  35.6 6.8 %collective-permute-start.3 = (bf16[6,1,64,128]{3,2,1,0:T(8,128)(2,1)S(1)}, bf16[6,1,64,128]{3,2,1,0:T(8,128)(2,1)S(1)}, u32[]{:S(2)}, u32[]{:S(2)}) collective-permute-start(bf16[6,1,64,128]{3,2,1,0:T(8,128)(2,1)S(1)} %get-tuple-element.8), channel_id=1, source_target_pairs={{1,0},{2,1},{3,2},{4,3},{5,4},{6,5},{7,6},{9,8},{10,9},{11,10},{12... | collective-permute-start | bytes 294920 | tf_op jit(solution)/shard_map/ppermute | solution.py:20
  44.6 1.2 copy-start.5
  45.5 12.4 %copy-start.1 = (bf16[6,18,64,384]{3,2,1,0:T(8,128)(2,1)}, bf16[6,18,64,384]{3,2,1,0:T(8,128)(2,1)S(1)}, u32[]{:S(2)}) copy-start(bf16[6,18,64,384]{3,2,1,0:T(8,128)(2,1)S(1)} %pad_maximum_fusion) | copy-start | bytes 15925252
  114.1 19.9 %all-to-all-start = ((bf16[64,2,256]{2,1,0:T(2,128)(2,1)}), bf16[64,2,256]{2,1,0:T(2,128)(2,1)}, u32[]{:S(2)}, u32[]{:S(2)}) async-start(bf16[64,2,256]{2,1,0:T(2,128)(2,1)} %reshape.950), calls=%async_computation | async-start | bytes 131072 | tf_op jit(solution)/shard_map/all_to_all | solution.py:72
  124.8 11.9 %copy-start.6 = (f32[1,2,256,64]{2,3,1,0:T(8,128)S(1)}, f32[1,2,256,64]{2,3,1,0:T(8,128)}, u32[]{:S(2)}) copy-start(f32[1,2,256,64]{2,3,1,0:T(8,128)} %get-tuple-element.15) | copy-start | bytes 393220
  138.8 15.7 %all-to-all-start.1 = ((bf16[2,256,1,1,128]{4,0,3,2,1:T(2,128)(2,1)}), bf16[2,256,1,1,128]{4,0,3,2,1:T(2,128)(2,1)S(1)}, u32[]{:S(2)}, u32[]{:S(2)}) async-start(bf16[2,256,1,1,128]{4,0,3,2,1:T(2,128)(2,1)} %copy.55), calls=%async_computation.1 | async-start | bytes 262144 | tf_op jit(solution)/shard_map/all_to_all | solution.py:87
  144.5 29.9 %copy-start.7 = (f32[1,2,16,16]{2,3,1,0:T(8,128)S(1)}, f32[1,2,16,16]{2,3,1,0:T(8,128)}, u32[]{:S(2)}) copy-start(f32[1,2,16,16]{2,3,1,0:T(8,128)} %get-tuple-element.19) | copy-start | bytes 6148
  148.7 26.4 %copy-start.8 = (bf16[1,16,64]{2,1,0:T(8,128)(2,1)S(1)}, bf16[1,16,64]{2,1,0:T(8,128)(2,1)}, u32[]{:S(2)}) copy-start(bf16[1,16,64]{2,1,0:T(8,128)(2,1)} %get-tuple-element.38) | copy-start | bytes 6148
  148.7 26.4 %copy-start.9 = (bf16[1,16,64]{2,1,0:T(8,128)(2,1)S(1)}, bf16[1,16,64]{2,1,0:T(8,128)(2,1)}, u32[]{:S(2)}) copy-start(bf16[1,16,64]{2,1,0:T(8,128)(2,1)} %get-tuple-element.39) | copy-start | bytes 6148
  154.7 20.8 %copy-start.2 = (f32[4,16,64,128]{3,2,1,0:T(8,128)S(1)}, f32[4,16,64,128]{3,2,1,0:T(8,128)}, u32[]{:S(2)}) copy-start(f32[4,16,64,128]{3,2,1,0:T(8,128)} %fusion.41) | copy-start | bytes 6291460
  154.7 20.8 %copy-start.3 = (f32[4,16,64,128]{3,2,1,0:T(8,128)S(1)}, f32[4,16,64,128]{3,2,1,0:T(8,128)}, u32[]{:S(2)}) copy-start(f32[4,16,64,128]{3,2,1,0:T(8,128)} %fusion.42) | copy-start | bytes 6291460
  154.7 20.8 %copy-start.10 = (f32[128]{0:T(128)S(1)}, f32[128]{0:T(128)}, u32[]{:S(2)}) copy-start(f32[128]{0:T(128)} %param.7) | copy-start | bytes 1540
Sparse Core Ops, SparseCore 0:
  22.4 87.7 all-reduce.3
where the time goes:
time: 192 us; the launch traced here: 191 us
  waiting for transfers between devices  64 us (33%)
  matrix products  36.8 us (19%)
  starting transfers between devices  33 us (17%)
  blocking collectives  19.6 us (10%)
  local copies, waits for them, and re-layouts  17.5 us (9%)
  between operations  13.8 us (7%)
  other arithmetic  6.65 us (3%)
    unnamed x2, waiting for transfers between devices  49.9 us
    dot_general x9, matrix products, convolve(): jnp.dot(stacked[shift_x:shift_x + cells_x, shift_y:shift_y + cells_y], ke...  31.7 us
    all_gather x1, blocking collectives, spectral_part(): lax.all_gather(summed.astype(jnp.bfloat16), 'gy', axis=2, tiled=True)  19.6 us
    ppermute x2, starting transfers between devices, with_halo(): before = lax.ppermute(last, axis, up)  12.5 us
    all_to_all x1, starting transfers between devices, spectral_part(): lax.all_to_all(owned_modes.astype(jnp.bfloat16), 'gx', split_axis=2, conc...  10.7 us
    unnamed x28, local copies, waits for them, and re-layouts  6.05 us
    all_to_all x1, waiting for transfers between devices, spectral_part(): lax.all_to_all(inverse_x.astype(jnp.bfloat16), 'gx', split_axis=1, concat...  5.77 us
    all_to_all x1, starting transfers between devices, spectral_part(): lax.all_to_all(inverse_x.astype(jnp.bfloat16), 'gx', split_axis=1, concat...  5.67 us
  transfers between devices with their start and end apart: 7, of which 4 were waited for; matrix products, arithmetic and copies ran while one was open for 21% of the time, Pallas kernels for 0%

commit v1 on v0

--- a/solution.py
+++ b/solution.py
@@ -90,9 +90,10 @@
     band_rows = MY // count_y
     summed = returned.reshape(2, cells_x, band_rows * MZ, 2, channels).sum(axis=3)
     summed = summed.reshape(2, cells_x, band_rows, MZ, channels)
-    coefficients = lax.all_gather(summed.astype(jnp.bfloat16), "gy", axis=2, tiled=True).astype(
-        summed.dtype
-    )
+    coefficients = jnp.concatenate(
+        lax.all_to_all(jnp.stack([summed.astype(jnp.bfloat16)] * lax.axis_size("gy")), "gy", 0, 0),
+        axis=2,
+    ).astype(summed.dtype)
     backward_y = complex_table(signed_modes(MY), local_y, full_y, MY ** (-0.5), 1.0)
     y_inverse = jnp.einsum("pxjkc,pqjy->qxykc", coefficients, backward_y, precision=highest).astype(
         jnp.bfloat16

time: 192 us -> 199 us (1.036)
  blocking collectives: 19.6 us -> 0 us
  waiting for transfers between devices: 64 us -> 74.6 us
  starting transfers between devices: 33 us -> 41.2 us
  matrix products: 36.8 us -> 41.3 us
  local copies, waits for them, and re-layouts: 17.5 us -> 20.2 us
    all_gather x1 -> x0, blocking collectives: 19.6 us -> none  [spectral_part(): lax.all_gather(summed.astype(jnp.bfloat16), 'gy', axis=2, tiled=True)]
    all_to_all x0 -> x1, starting transfers between devices: none -> 8.22 us  [spectral_part(): lax.all_to_all(jnp.stack([summed.astype(jnp.bfloat16)] * lax.axis_size('g...]
    unnamed x2, waiting for transfers between devices: 49.9 us -> 57 us
    dot_general x9, matrix products: 31.7 us -> 36.3 us  [convolve(): jnp.dot(stacked[shift_x:shift_x + cells_x, shift_y:shift_y + cells_y], ke...]
    all_to_all x0 -> x1, waiting for transfers between devices: none -> 3.72 us  [spectral_part(): lax.all_to_all(jnp.stack([summed.astype(jnp.bfloat16)] * lax.axis_size('g...]
    unnamed x28 -> x32, local copies, waits for them, and re-layouts: 6.05 us -> 6.66 us
  transfers between devices with their start and end apart: 7 -> 8, of which waited for: 4 -> 5; matrix products, arithmetic and copies ran while one was open for 21% -> 22% of each run, Pallas kernels for 0% -> 0%
where the time goes in v1:
time: 199 us; the launch traced here: 198 us
  waiting for transfers between devices  74.6 us (37%)
  matrix products  41.3 us (21%)
  starting transfers between devices  41.2 us (21%)
  local copies, waits for them, and re-layouts  20.2 us (10%)
  between operations  13.7 us (7%)
  other arithmetic  6.63 us (3%)
    unnamed x2, waiting for transfers between devices  57 us
    dot_general x9, matrix products, convolve(): jnp.dot(stacked[shift_x:shift_x + cells_x, shift_y:shift_y + cells_y], ke...  36.3 us
    ppermute x2, starting transfers between devices, with_halo(): before = lax.ppermute(last, axis, up)  12.4 us
    all_to_all x1, starting transfers between devices, spectral_part(): lax.all_to_all(owned_modes.astype(jnp.bfloat16), 'gx', split_axis=2, conc...  10.7 us
    all_to_all x1, starting transfers between devices, spectral_part(): lax.all_to_all(jnp.stack([summed.astype(jnp.bfloat16)] * lax.axis_size('g...  8.22 us
    unnamed x32, local copies, waits for them, and re-layouts  6.66 us
    all_to_all x1, waiting for transfers between devices, spectral_part(): lax.all_to_all(inverse_x.astype(jnp.bfloat16), 'gx', split_axis=1, concat...  5.81 us
    all_to_all x1, starting transfers between devices, spectral_part(): lax.all_to_all(inverse_x.astype(jnp.bfloat16), 'gx', split_axis=1, concat...  5.71 us
  transfers between devices with their start and end apart: 8, of which 5 were waited for; matrix products, arithmetic and copies ran while one was open for 22% of the time, Pallas kernels for 0%

profile of v1, /device:TPU:1, one launch (start us, length us, event | category | flops | bytes accessed | tf_op | source)
XLA Modules:
  0.0 197.7 jit_solution(10743018874617079695)
XLA Ops:
  6.5 2.0 %fusion.100 = (bf16[1,16,64,128]{3,2,1,0:T(8,128)(2,1)}, bf16[1,16,64,128]{3,2,1,0:T(8,128)(2,1)}) fusion(bf16[4,16,64,128]{3,2,1,0:T(8,128)(2,1)} %param.4), kind=kLoop, calls=%fused_computation.177 | loop fusion | bytes 1048576 | tf_op jit(solution)/shard_map/slice | solution.py:18
  9.8 5.4 %collective-permute-start = (bf16[1,16,64,128]{3,2,1,0:T(8,128)(2,1)}, bf16[1,16,64,128]{3,2,1,0:T(8,128)(2,1)}, u32[]{:S(2)}, u32[]{:S(2)}) collective-permute-start(bf16[1,16,64,128]{3,2,1,0:T(8,128)(2,1)} %get-tuple-element.10), channel_id=1, source_target_pairs={{0,8},{8,16},{16,24},{24,32},{32,40},{40,48},{48,56},{56,64},{64,7... | collective-permute-start | bytes 786440 | tf_op jit(solution)/shard_map/ppermute | solution.py:19
  19.7 2.5 %convert_element_type.206 = bf16[2,4,8,64,1,64]{5,3,2,1,0,4:T(8,128)(2,1)} reshape(bf16[2,4,16,16,128]{4,3,2,1,0:T(8,128)(2,1)} %copy.18) | data formatting | bytes 1048576 | tf_op jit(solution)/shard_map/convert_element_type | solution.py:69
  28.4 7.1 %collective-permute-start.2 = (bf16[6,1,64,128]{3,2,1,0:T(8,128)(2,1)S(1)}, bf16[6,1,64,128]{3,2,1,0:T(8,128)(2,1)S(1)}, u32[]{:S(2)}, u32[]{:S(2)}) collective-permute-start(bf16[6,1,64,128]{3,2,1,0:T(8,128)(2,1)S(1)} %get-tuple-element.7), channel_id=1, source_target_pairs={{0,1},{1,2},{2,3},{3,4},{4,5},{5,6},{6,7},{8,9},{9,10},{10,11},{11... | collective-permute-start | bytes 294920 | tf_op jit(solution)/shard_map/ppermute | solution.py:19
  35.5 2.9 %collective-permute-start.3 = (bf16[6,1,64,128]{3,2,1,0:T(8,128)(2,1)S(1)}, bf16[6,1,64,128]{3,2,1,0:T(8,128)(2,1)S(1)}, u32[]{:S(2)}, u32[]{:S(2)}) collective-permute-start(bf16[6,1,64,128]{3,2,1,0:T(8,128)(2,1)S(1)} %get-tuple-element.8), channel_id=1, source_target_pairs={{1,0},{2,1},{3,2},{4,3},{5,4},{6,5},{7,6},{9,8},{10,9},{11,10},{12... | collective-permute-start | bytes 294920 | tf_op jit(solution)/shard_map/ppermute | solution.py:20
  39.1 3.3 %collective-permute-done.3 = bf16[6,1,64,128]{3,2,1,0:T(8,128)(2,1)S(1)} collective-permute-done((bf16[6,1,64,128]{3,2,1,0:T(8,128)(2,1)S(1)}, bf16[6,1,64,128]{3,2,1,0:T(8,128)(2,1)S(1)}, u32[]{:S(2)}, u32[]{:S(2)}) %collective-permute-start.3) | collective-permute-done | bytes 98336 | tf_op jit(solution)/shard_map/ppermute | solution.py:20
  45.7 2.6 %fusion.41 = f32[4,16,64,128]{3,2,1,0:T(8,128)} fusion(bf16[6,18,64,384]{3,2,1,0:T(8,128)(2,1)S(1)} %pad_maximum_fusion, bf16[3,3,384,128]{3,2,1,0:T(8,128)(2,1)S(1)} %bitcast.232), kind=kOutput, calls=%fused_computation.56 | convolution fusion | flops 402653184 | bytes 7503872 | tf_op jit(solution)/shard_map/dot_general | solution.py:117
  48.4 2.3 %fusion.42 = f32[4,16,64,128]{3,2,1,0:T(8,128)} fusion(bf16[6,18,64,384]{3,2,1,0:T(8,128)(2,1)S(1)} %pad_maximum_fusion, bf16[3,3,384,128]{3,2,1,0:T(8,128)(2,1)S(1)} %bitcast.233), kind=kOutput, calls=%fused_computation.58 | convolution fusion | flops 402653184 | bytes 7503872 | tf_op jit(solution)/shard_map/dot_general | solution.py:117
  50.7 2.4 %fusion.43 = f32[4,16,64,128]{3,2,1,0:T(8,128)} fusion(bf16[6,18,64,384]{3,2,1,0:T(8,128)(2,1)S(1)} %pad_maximum_fusion, bf16[3,3,384,128]{3,2,1,0:T(8,128)(2,1)S(1)} %bitcast.234), kind=kOutput, calls=%fused_computation.60 | convolution fusion | flops 402653184 | bytes 7503872 | tf_op jit(solution)/shard_map/dot_general | solution.py:117
  53.0 57.0 %all-reduce.4.cloned.1.call-done = bf16[2,4,8,64,1,64]{5,3,2,1,0,4:T(8,128)(2,1)} async-done(((bf16[2,4,8,64,1,64]{5,3,2,1,0,4:T(8,128)(2,1)}), bf16[2,4,8,64,1,64]{5,3,2,1,0,4:T(8,128)(2,1)}) %all-reduce.4.cloned.1.call-update) | async-done | bytes 524304
  112.3 1.7 reshape.961
  114.0 10.7 %all-to-all-start = ((bf16[64,2,256]{2,1,0:T(2,128)(2,1)}), bf16[64,2,256]{2,1,0:T(2,128)(2,1)}, u32[]{:S(2)}, u32[]{:S(2)}) async-start(bf16[64,2,256]{2,1,0:T(2,128)(2,1)} %reshape.961), calls=%async_computation | async-start | bytes 131072 | tf_op jit(solution)/shard_map/all_to_all | solution.py:72
  124.7 4.3 %fusion.44 = f32[4,16,64,128]{3,2,1,0:T(8,128)} fusion(bf16[6,18,64,384]{3,2,1,0:T(8,128)(2,1)} %copy-done.1, bf16[3,3,384,128]{3,2,1,0:T(8,128)(2,1)S(1)} %bitcast.235), kind=kOutput, calls=%fused_computation.62 | convolution fusion | flops 402653184 | bytes 7503872 | tf_op jit(solution)/shard_map/dot_general | solution.py:117
  129.0 4.7 %all-to-all-done = bf16[64,2,256]{2,1,0:T(2,128)(2,1)} async-done(((bf16[64,2,256]{2,1,0:T(2,128)(2,1)}), bf16[64,2,256]{2,1,0:T(2,128)(2,1)}, u32[]{:S(2)}, u32[]{:S(2)}) %all-to-all-start) | async-done | bytes 65568 | tf_op jit(solution)/shard_map/all_to_all | solution.py:72
  133.7 1.7 reshape.962
  138.6 5.7 %all-to-all-start.1 = ((bf16[2,256,1,1,128]{4,0,3,2,1:T(2,128)(2,1)}), bf16[2,256,1,1,128]{4,0,3,2,1:T(2,128)(2,1)S(1)}, u32[]{:S(2)}, u32[]{:S(2)}) async-start(bf16[2,256,1,1,128]{4,0,3,2,1:T(2,128)(2,1)} %copy.25), calls=%async_computation.1 | async-start | bytes 262144 | tf_op jit(solution)/shard_map/all_to_all | solution.py:87
  144.3 4.2 %fusion.45 = f32[4,16,64,128]{3,2,1,0:T(8,128)} fusion(bf16[6,18,64,384]{3,2,1,0:T(8,128)(2,1)} %copy-done.1, bf16[3,3,384,128]{3,2,1,0:T(8,128)(2,1)S(1)} %bitcast.236), kind=kOutput, calls=%fused_computation.64 | convolution fusion | flops 402653184 | bytes 7503872 | tf_op jit(solution)/shard_map/dot_general | solution.py:117
  148.5 5.8 %all-to-all-done.1 = bf16[2,256,1,1,128]{4,0,3,2,1:T(2,128)(2,1)S(1)} async-done(((bf16[2,256,1,1,128]{4,0,3,2,1:T(2,128)(2,1)}), bf16[2,256,1,1,128]{4,0,3,2,1:T(2,128)(2,1)S(1)}, u32[]{:S(2)}, u32[]{:S(2)}) %all-to-all-start.1) | async-done | bytes 131104 | tf_op jit(solution)/shard_map/all_to_all | solution.py:87
  155.4 8.2 %all-to-all-start.2 = ((bf16[8,2,4,2,16,128]{5,4,3,2,1,0:T(8,128)(2,1)}), bf16[8,2,4,2,16,128]{5,4,3,2,1,0:T(8,128)(2,1)}, u32[]{:S(2)}, u32[]{:S(2)}) async-start(bf16[8,2,4,2,16,128]{5,4,3,2,1,0:T(8,128)(2,1)} %stack.127), calls=%async_computation.2 | async-start | bytes 1048576 | tf_op jit(solution)/shard_map/all_to_all | solution.py:94
  163.7 4.3 %fusion.46 = f32[4,16,64,128]{3,2,1,0:T(8,128)} fusion(bf16[6,18,64,384]{3,2,1,0:T(8,128)(2,1)} %copy-done.1, bf16[3,3,384,128]{3,2,1,0:T(8,128)(2,1)} %bitcast.228), kind=kOutput, calls=%fused_computation.66 | convolution fusion | flops 402653184 | bytes 7503872 | tf_op jit(solution)/shard_map/dot_general | solution.py:117
  168.0 4.2 %fusion.47 = f32[4,16,64,128]{3,2,1,0:T(8,128)} fusion(bf16[6,18,64,384]{3,2,1,0:T(8,128)(2,1)} %copy-done.1, bf16[3,3,384,128]{3,2,1,0:T(8,128)(2,1)} %bitcast.229), kind=kOutput, calls=%fused_computation.68 | convolution fusion | flops 402653184 | bytes 7503872 | tf_op jit(solution)/shard_map/dot_general | solution.py:117
  172.2 3.2 %fusion.48 = f32[4,16,64,128]{3,2,1,0:T(8,128)} fusion(bf16[6,18,64,384]{3,2,1,0:T(8,128)(2,1)S(1)} %bitcast.226, bf16[3,3,384,128]{3,2,1,0:T(8,128)(2,1)} %bitcast.230), kind=kOutput, calls=%fused_computation.70 | convolution fusion | flops 402653184 | bytes 7503872 | tf_op jit(solution)/shard_map/dot_general | solution.py:117
  175.4 3.7 %all-to-all-done.2 = bf16[8,2,4,2,16,128]{5,4,3,2,1,0:T(8,128)(2,1)} async-done(((bf16[8,2,4,2,16,128]{5,4,3,2,1,0:T(8,128)(2,1)}), bf16[8,2,4,2,16,128]{5,4,3,2,1,0:T(8,128)(2,1)}, u32[]{:S(2)}, u32[]{:S(2)}) %all-to-all-start.2) | async-done | bytes 524320 | tf_op jit(solution)/shard_map/all_to_all | solution.py:94
  182.1 8.8 %fusion.11 = bf16[4,16,64,128]{3,2,1,0:T(8,128)(2,1)} fusion(f32[64,4,16,128,1]{3,0,4,2,1:T(8,128)S(1)} %fusion.32, f32[4,16,64,128]{3,2,1,0:T(8,128)S(1)} %copy-done.2, f32[4,16,64,128]{3,2,1,0:T(8,128)S(1)} %copy-done.3, f32[4,16,64,128]{3,2,1,0:T(8,128)} %fusion.43, f32[4,16,64,128]{3,2,1,0:T(8,128)} %fusion.44, f32[4,16,64,128]{3,2,1,0:T(8,128)} %fusion.45, ...), kind=kOutput, calls=%fused_computation.15 | convolution fusion | flops 412614656 | bytes 25330176 | tf_op jit(solution)/shard_map/dot_general | solution.py:117
  (72 shorter events, 25.4 us)
Async XLA Ops:
  6.5 130.1 %copy-start = (bf16[1,64,2,64,128]{4,3,2,1,0:T(8,128)(2,1)S(1)}, bf16[1,64,2,64,128]{4,3,2,1,0:T(8,128)(2,1)}, u32[]{:S(2)}) copy-start(bf16[1,64,2,64,128]{4,3,2,1,0:T(8,128)(2,1)} %param.5) | copy-start | bytes 6291460
  6.5 103.5 %all-reduce.4.cloned.1.call-start = ((), (), s32[]{:S(2)}) async-start(), calls=%async_computation.3 | async-start | bytes 2097152
  8.6 18.9 %collective-permute-start.1 = (bf16[1,16,64,128]{3,2,1,0:T(8,128)(2,1)}, bf16[1,16,64,128]{3,2,1,0:T(8,128)(2,1)}, u32[]{:S(2)}, u32[]{:S(2)}) collective-permute-start(bf16[1,16,64,128]{3,2,1,0:T(8,128)(2,1)} %get-tuple-element.9), channel_id=1, source_target_pairs={{8,0},{16,8},{24,16},{32,24},{40,32},{48,40},{56,48},{64,56},{72,6... | collective-permute-start | bytes 786440 | tf_op jit(solution)/shard_map/ppermute | solution.py:20
  9.8 16.5 %collective-permute-start = (bf16[1,16,64,128]{3,2,1,0:T(8,128)(2,1)}, bf16[1,16,64,128]{3,2,1,0:T(8,128)(2,1)}, u32[]{:S(2)}, u32[]{:S(2)}) collective-permute-start(bf16[1,16,64,128]{3,2,1,0:T(8,128)(2,1)} %get-tuple-element.10), channel_id=1, source_target_pairs={{0,8},{8,16},{16,24},{24,32},{32,40},{40,48},{48,56},{56,64},{64,7... | collective-permute-start | bytes 786440 | tf_op jit(solution)/shard_map/ppermute | solution.py:19
  19.7 7.5 %copy-start.4 = (bf16[4,16,64,128]{3,2,1,0:T(8,128)(2,1)S(1)}, bf16[4,16,64,128]{3,2,1,0:T(8,128)(2,1)}, u32[]{:S(2)}) copy-start(bf16[4,16,64,128]{3,2,1,0:T(8,128)(2,1)} %param.4) | copy-start | bytes 3145732
  28.4 10.6 %collective-permute-start.2 = (bf16[6,1,64,128]{3,2,1,0:T(8,128)(2,1)S(1)}, bf16[6,1,64,128]{3,2,1,0:T(8,128)(2,1)S(1)}, u32[]{:S(2)}, u32[]{:S(2)}) collective-permute-start(bf16[6,1,64,128]{3,2,1,0:T(8,128)(2,1)S(1)} %get-tuple-element.7), channel_id=1, source_target_pairs={{0,1},{1,2},{2,3},{3,4},{4,5},{5,6},{6,7},{8,9},{9,10},{10,11},{11... | collective-permute-start | bytes 294920 | tf_op jit(solution)/shard_map/ppermute | solution.py:19
  35.5 6.8 %collective-permute-start.3 = (bf16[6,1,64,128]{3,2,1,0:T(8,128)(2,1)S(1)}, bf16[6,1,64,128]{3,2,1,0:T(8,128)(2,1)S(1)}, u32[]{:S(2)}, u32[]{:S(2)}) collective-permute-start(bf16[6,1,64,128]{3,2,1,0:T(8,128)(2,1)S(1)} %get-tuple-element.8), channel_id=1, source_target_pairs={{1,0},{2,1},{3,2},{4,3},{5,4},{6,5},{7,6},{9,8},{10,9},{11,10},{12... | collective-permute-start | bytes 294920 | tf_op jit(solution)/shard_map/ppermute | solution.py:20
  44.6 1.2 copy-start.5
  45.4 5.2 %copy-start.1 = (bf16[6,18,64,384]{3,2,1,0:T(8,128)(2,1)}, bf16[6,18,64,384]{3,2,1,0:T(8,128)(2,1)S(1)}, u32[]{:S(2)}) copy-start(bf16[6,18,64,384]{3,2,1,0:T(8,128)(2,1)S(1)} %pad_maximum_fusion) | copy-start | bytes 15925252
  114.0 19.7 %all-to-all-start = ((bf16[64,2,256]{2,1,0:T(2,128)(2,1)}), bf16[64,2,256]{2,1,0:T(2,128)(2,1)}, u32[]{:S(2)}, u32[]{:S(2)}) async-start(bf16[64,2,256]{2,1,0:T(2,128)(2,1)} %reshape.961), calls=%async_computation | async-start | bytes 131072 | tf_op jit(solution)/shard_map/all_to_all | solution.py:72
  124.7 11.7 %copy-start.6 = (f32[1,2,256,64]{2,3,1,0:T(8,128)S(1)}, f32[1,2,256,64]{2,3,1,0:T(8,128)}, u32[]{:S(2)}) copy-start(f32[1,2,256,64]{2,3,1,0:T(8,128)} %get-tuple-element.15) | copy-start | bytes 393220
  138.6 15.7 %all-to-all-start.1 = ((bf16[2,256,1,1,128]{4,0,3,2,1:T(2,128)(2,1)}), bf16[2,256,1,1,128]{4,0,3,2,1:T(2,128)(2,1)S(1)}, u32[]{:S(2)}, u32[]{:S(2)}) async-start(bf16[2,256,1,1,128]{4,0,3,2,1:T(2,128)(2,1)} %copy.25), calls=%async_computation.1 | async-start | bytes 262144 | tf_op jit(solution)/shard_map/all_to_all | solution.py:87
  155.4 16.8 %slice-start = ((s8[5308416]{0:T(1024)(128)(4,1)}), s8[1114112]{0:T(1024)(128)(4,1)S(1)}, s32[]{:S(2)}) async-start(s8[5308416]{0:T(1024)(128)(4,1)} %bitcast.225), calls=%async_computation.4 | async-start | bytes 2228224
  155.4 23.7 %all-to-all-start.2 = ((bf16[8,2,4,2,16,128]{5,4,3,2,1,0:T(8,128)(2,1)}), bf16[8,2,4,2,16,128]{5,4,3,2,1,0:T(8,128)(2,1)}, u32[]{:S(2)}, u32[]{:S(2)}) async-start(bf16[8,2,4,2,16,128]{5,4,3,2,1,0:T(8,128)(2,1)} %stack.127), calls=%async_computation.2 | async-start | bytes 1048576 | tf_op jit(solution)/shard_map/all_to_all | solution.py:94
  163.7 8.6 %slice-start.1 = ((s8[5308416]{0:T(1024)(128)(4,1)}), s8[4194304]{0:T(1024)(128)(4,1)S(1)}, s32[]{:S(2)}) async-start(s8[5308416]{0:T(1024)(128)(4,1)} %bitcast.225), calls=%async_computation.5 | async-start | bytes 8388608
  172.2 8.2 %copy-start.7 = (f32[1,2,16,16]{2,3,1,0:T(8,128)S(1)}, f32[1,2,16,16]{2,3,1,0:T(8,128)}, u32[]{:S(2)}) copy-start(f32[1,2,16,16]{2,3,1,0:T(8,128)} %get-tuple-element.19) | copy-start | bytes 6148
  175.4 5.6 %copy-start.8 = (bf16[1,16,64]{2,1,0:T(8,128)(2,1)S(1)}, bf16[1,16,64]{2,1,0:T(8,128)(2,1)}, u32[]{:S(2)}) copy-start(bf16[1,16,64]{2,1,0:T(8,128)(2,1)} %get-tuple-element.38) | copy-start | bytes 6148
  175.4 5.6 %copy-start.9 = (bf16[1,16,64]{2,1,0:T(8,128)(2,1)S(1)}, bf16[1,16,64]{2,1,0:T(8,128)(2,1)}, u32[]{:S(2)}) copy-start(bf16[1,16,64]{2,1,0:T(8,128)(2,1)} %get-tuple-element.39) | copy-start | bytes 6148
  179.1 2.4 %copy-start.3 = (f32[4,16,64,128]{3,2,1,0:T(8,128)S(1)}, f32[4,16,64,128]{3,2,1,0:T(8,128)}, u32[]{:S(2)}) copy-start(f32[4,16,64,128]{3,2,1,0:T(8,128)} %fusion.42) | copy-start | bytes 6291460
  180.4 1.7 copy-start.2
  180.4 1.7 copy-start.10
Sparse Core Ops, SparseCore 0:
  22.3 87.6 all-reduce.3
